TPU v7x, 128 devices: a whole 4x4x4 slice. The times are simulated.
128 devices in a mesh: dp: 2 (over core), row: 4 (over x), col: 16 (over z, y).
Axes of the slice: x: 4, y: 4, z: 4, core: 2. Of those that a mesh axis runs over, the one named last changes fastest.
Arguments:
- forget_tokens: bfloat16 [256, 6144], P('dp', 'col'), may hold values from -6 to 6
- forget_cotangent: bfloat16 [256, 6144], P('dp', 'col'), may hold values from -6 to 6
- forget_labels: int32 [256], P('dp'), may hold values 0 or 1
- retain_tokens: bfloat16 [256, 6144], P('dp', 'col'), may hold values from -6 to 6
- ln_gain: float32 [6144], P('col'), may hold values from 0.25 to 1.75
- w_in: bfloat16 [6144, 24576], P('col', 'row'), may hold values from -0.078125 to 0.078125
- b_in: float32 [24576], P('row'), may hold values from -3 to 3
- w_out: bfloat16 [24576, 6144], P('row', 'col'), may hold values from -0.0390625 to 0.0390625
- b_out: float32 [6144], P('col'), may hold values from -3 to 3
- pruned: int32 [512], P('row'), may hold values from 0 to 24575, as said below
Outputs:
- saliency: float32 [24576], P('row')
- retain_out: bfloat16 [256, 6144], P(('dp', 'row'), 'col')
Inputs may be any that keep to these rules, and one draw needn't show every extreme that they name: `pruned`: entries r * 128 to (r + 1) * 128 - 1 are distinct neurons that all lie in the r-th of the equal neuron ranges of the row shards.
All inputs are finite; a program needn't handle non-finite values. No bound on the sum of `forget_labels` on one device may be relied on, other than what follows from the above.
Results may differ from a plain program's by a relative error of at most 0.0052.
Values may be sent and summed in bfloat16 or wider, within the bound.
No kernel may reach another device: no remote copies, remote signals or barrier semaphores. Data moves between devices by JAX's collectives and lax.ppermute only.
A program may use at most 128 MiB of HBM per device.

v0:
```python
import jax
import jax.numpy as jnp
from jax import lax
from jax.sharding import PartitionSpec as P

D = 6144


def gelu_exact(v):
    return v * 0.5 * (1.0 + lax.erf(v * 0.7071067811865476))


def gelu_slope(v):
    return (
        0.5 * (1.0 + lax.erf(v * 0.7071067811865476))
        + v * jnp.exp(-0.5 * v * v) * 0.3989422804014327
    )


def outer_rows(left, right):
    return lax.dot_general(
        left, right, (((0,), (0,)), ((), ())), preferred_element_type=jnp.float32
    )


def local(
    forget_tokens,
    forget_cotangent,
    forget_labels,
    retain_tokens,
    ln_gain,
    w_in,
    b_in,
    w_out,
    b_out,
    pruned,
):
    forget_rows = forget_tokens.shape[0]
    width_local = w_in.shape[0]
    neurons_local = w_in.shape[1]
    joined = jnp.concatenate([forget_tokens, retain_tokens], axis=0).astype(jnp.float32)
    mean_val = lax.psum(jnp.sum(joined, axis=1, keepdims=True), "col") / D
    centred = joined - mean_val
    var_val = lax.psum(jnp.sum(centred * centred, axis=1, keepdims=True), "col") / D
    normed = (centred * lax.rsqrt(var_val + 1e-06) * ln_gain).astype(jnp.bfloat16)
    partial_pre = jnp.dot(normed, w_in, preferred_element_type=jnp.float32)
    grad_y = forget_cotangent * forget_labels[:, None].astype(jnp.bfloat16)
    grad_part = lax.dot_general(
        grad_y, w_out, (((1,), (1,)), ((), ())), preferred_element_type=jnp.float32
    )
    share_width = neurons_local // lax.axis_size("col")
    share_start = lax.axis_index("col") * share_width
    bias_share = lax.dynamic_slice_in_dim(b_in, share_start, share_width, 0)
    pre_share = lax.psum_scatter(partial_pre, "col", scatter_dimension=1, tiled=True) + bias_share
    act_share = gelu_exact(pre_share).astype(jnp.bfloat16)
    act_all = lax.all_gather(act_share, "col", axis=1, tiled=True)
    grad_act_share = lax.psum_scatter(
        grad_part.astype(jnp.bfloat16), "col", scatter_dimension=1, tiled=True
    ).astype(jnp.float32)
    grad_pre_share = (grad_act_share * gelu_slope(pre_share[:forget_rows])).astype(jnp.bfloat16)
    grad_pre = lax.all_gather(grad_pre_share, "col", axis=1, tiled=True)
    act_f = act_all[:forget_rows]
    act_r = act_all[forget_rows:]
    normed_f = normed[:forget_rows]
    local_in = outer_rows(normed_f, grad_pre)
    local_out = outer_rows(act_f, grad_y)
    summed_in, summed_out = (
        lax.psum_scatter(
            local_in.astype(jnp.bfloat16), "dp", scatter_dimension=0, tiled=True
        ).astype(jnp.float32),
        lax.psum_scatter(
            local_out.astype(jnp.bfloat16), "dp", scatter_dimension=1, tiled=True
        ).astype(jnp.float32),
    )
    slice_rows = width_local // lax.axis_size("dp")
    slice_start = lax.axis_index("dp") * slice_rows
    weight_in_rows = lax.dynamic_slice_in_dim(w_in, slice_start, slice_rows, 0).astype(jnp.float32)
    weight_out_cols = lax.dynamic_slice_in_dim(w_out, slice_start, slice_rows, 1).astype(
        jnp.float32
    )
    terms = jnp.sum(jnp.abs(weight_in_rows * summed_in), axis=0) + jnp.sum(
        jnp.abs(weight_out_cols * summed_out), axis=1
    )
    saliency = lax.psum(terms, ("dp", "col")) / D
    neuron_ids = lax.axis_index("row") * neurons_local + jnp.arange(neurons_local, dtype=jnp.int32)
    is_pruned = jnp.any(pruned[:, None] == neuron_ids[None, :], axis=0)
    keep = jnp.where(is_pruned, 0.0, 1.0).astype(jnp.bfloat16)
    masked_r = act_r * keep[None, :]
    out_part = jnp.dot(masked_r, w_out, preferred_element_type=jnp.float32)
    retain_out = (
        lax.psum_scatter(out_part, "row", scatter_dimension=0, tiled=True) + b_out
    ).astype(jnp.bfloat16)
    return (saliency, retain_out)


def solution(mesh):
    in_specs = (
        P("dp", "col"),
        P("dp", "col"),
        P("dp"),
        P("dp", "col"),
        P("col"),
        P("col", "row"),
        P("row"),
        P("row", "col"),
        P("col"),
        P("row"),
    )
    out_specs = (P("row"), P(("dp", "row"), "col"))
    return jax.shard_map(local, mesh=mesh, in_specs=in_specs, out_specs=out_specs, check_vma=False)
```

profile of v0, /device:TPU:1, one launch (start us, length us, event | category | flops | bytes accessed | tf_op | source)
XLA Modules:
  0.0 550.1 jit_solution(13570674265357662978)
XLA Ops:
  7.2 0.0 reduce-scatter.8.cloned.1.call-start
  7.2 1.1 convert_reduce_fusion
  8.3 35.5 %psum.21 = f32[256,1]{0,1:T(1,128)S(1)} all-reduce(f32[256,1]{0,1:T(1,128)S(1)} %bitcast.16), channel_id=1, replica_groups=mesh['dp'=2,'row'=4,'col'=16] {'col'}, use_global_device_ids=true, to_apply=%region_1.0 | all-reduce | flops 256 | bytes 2048 | tf_op jit(solution)/shard_map/psum | solution.py:42
  43.8 1.1 fusion.5
  44.9 28.5 %psum.22 = f32[256,1]{0,1:T(1,128)S(1)} all-reduce(f32[256,1]{0,1:T(1,128)S(1)} %bitcast.17), channel_id=1, replica_groups=mesh['dp'=2,'row'=4,'col'=16] {'col'}, use_global_device_ids=true, to_apply=%region_3.0 | all-reduce | flops 256 | bytes 2048 | tf_op jit(solution)/shard_map/psum | solution.py:44
  73.5 1.1 fusion.7
  74.6 6.8 %fusion.19 = f32[256,6144]{1,0:T(8,128)} fusion(bf16[256,384]{1,0:T(8,128)(2,1)S(1)} %fusion.7, bf16[384,6144]{1,0:T(8,128)(2,1)} %param.15), kind=kOutput, calls=%fused_computation.39 | convolution fusion | flops 1207959552 | bytes 11206656 | tf_op jit(solution)/shard_map/dot_general | solution.py:46
  81.4 0.0 reduce-scatter.8.cloned.1.call-update
  81.4 0.0 reduce-scatter.16.cloned.1.call-start
  81.4 0.6 copy-done.5
  82.0 0.2 copy-done.2
  82.3 3.9 convolution_convert_fusion.2
  86.2 0.0 copy-start.4
  86.2 1.7 copy.16
  87.9 0.0 reduce-scatter.16.cloned.1.call-update
  87.9 0.0 all-gather.5.cloned.1.call-start
  88.0 0.8 dynamic_slice.10
  88.8 85.5 %reduce-scatter.8.cloned.1.call-done = f32[256,384]{1,0:T(8,128)} async-done(((f32[256,6144]{1,0:T(8,128)}), f32[256,384]{1,0:T(8,128)}) %reduce-scatter.8.cloned.1.call-update) | async-done | bytes 393232 | tf_op jit(solution)/shard_map/reduce_scatter | solution.py:54
  174.2 1.8 multiply_convert_fusion
  176.0 0.0 all-gather.5.cloned.1.call-update
  176.0 0.0 all-gather.3.cloned.1.call-start
  176.1 73.9 %reduce-scatter.16.cloned.1.call-done = bf16[384,128]{1,0:T(8,128)(2,1)} async-done(((bf16[6144,128]{1,0:T(8,128)(2,1)}), bf16[384,128]{1,0:T(8,128)(2,1)}) %reduce-scatter.16.cloned.1.call-update) | async-done | bytes 98320
  249.9 1.0 copy.17
  250.9 0.7 fusion.13
  251.7 0.0 all-gather.3.cloned.1.call-update
  251.7 0.0 reduce-scatter.14.cloned.1.call-start
  251.8 0.5 compare_reduce_fusion
  252.3 52.4 %all-gather.5.cloned.1.call-done = bf16[256,6144]{1,0:T(8,128)(2,1)} async-done(((bf16[256,384]{1,0:T(8,128)(2,1)}), bf16[256,6144]{1,0:T(8,128)(2,1)}) %all-gather.5.cloned.1.call-update) | async-done | bytes 3145744 | tf_op jit(solution)/shard_map/all_gather | solution.py:56
  304.7 4.5 fusion
  309.2 0.0 reduce-scatter.14.cloned.1.call-update
  309.2 0.0 reduce-scatter.10.cloned.1.call-start
  309.3 41.8 %all-gather.3.cloned.1.call-done = bf16[128,6144]{1,0:T(8,128)(2,1)} async-done(((bf16[128,384]{1,0:T(8,128)(2,1)}), bf16[128,6144]{1,0:T(8,128)(2,1)}) %all-gather.3.cloned.1.call-update) | async-done | bytes 1572880 | tf_op jit(solution)/shard_map/all_gather | solution.py:61
  351.1 4.9 convolution_convert_fusion.1
  356.0 0.0 reduce-scatter.10.cloned.1.call-update
  356.1 0.0 reduce-scatter.12.cloned.1.call-start
  356.1 1.8 copy-done.1
  357.9 3.7 convolution_convert_fusion
  361.6 0.0 reduce-scatter.12.cloned.1.call-update
  361.6 3.6 constant_dynamic-slice_fusion
  365.2 2.7 copy.18
  367.9 4.1 reduce-scatter.14.cloned.1.call-done
  372.0 1.4 add_convert_fusion
  373.4 18.7 %reduce-scatter.10.cloned.1.call-done = bf16[192,6144]{1,0:T(8,128)(2,1)} async-done(((bf16[384,6144]{1,0:T(8,128)(2,1)}), bf16[192,6144]{1,0:T(8,128)(2,1)}) %reduce-scatter.10.cloned.1.call-update) | async-done | bytes 2359312 | tf_op jit(solution)/shard_map/reduce_scatter | solution.py:68
  392.2 3.2 abs_reduce_fusion.1
  395.3 15.9 %reduce-scatter.12.cloned.1.call-done = bf16[6144,192]{0,1:T(8,128)(2,1)} async-done(((bf16[6144,384]{0,1:T(8,128)(2,1)}), bf16[6144,192]{0,1:T(8,128)(2,1)}) %reduce-scatter.12.cloned.1.call-update) | async-done | bytes 2359312 | tf_op jit(solution)/shard_map/reduce_scatter | solution.py:71
  411.2 2.5 abs_reduce_fusion
  413.7 128.9 %psum.23 = f32[6144]{0:T(1024)S(1)} all-reduce(f32[6144]{0:T(1024)S(1)} %add.84), channel_id=1, replica_groups=mesh['dp'=2,'row'=4,'col'=16] {'dp','col'}, use_global_device_ids=true, to_apply=%region_10.0 | all-reduce | flops 6144 | bytes 49152 | tf_op jit(solution)/shard_map/psum | solution.py:84
  542.6 0.6 broadcast_multiply_fusion
  (14 shorter events, 0.1 us)
Async XLA Ops:
  7.2 167.1 %reduce-scatter.8.cloned.1.call-start = ((), (), s32[]{:S(2)}) async-start(), calls=%async_computation.5 | async-start | bytes 6684672 | tf_op jit(solution)/shard_map/reduce_scatter | solution.py:54
  81.4 0.7 copy-start.5
  81.4 0.9 copy-start.2
  81.4 168.5 %reduce-scatter.16.cloned.1.call-start = ((), (), s32[]{:S(2)}) async-start(), calls=%async_computation.11 | async-start | bytes 1671168
  86.2 165.5 %copy-start.4 = (s32[128]{0:T(128)S(1)}, s32[128]{0:T(128)}, u32[]{:S(2)}) copy-start(s32[128]{0:T(128)} %param.19) | copy-start | bytes 1540
  87.9 216.8 %all-gather.5.cloned.1.call-start = ((), (), s32[]{:S(2)}) async-start(), calls=%async_computation.8 | async-start | bytes 3342336 | tf_op jit(solution)/shard_map/all_gather | solution.py:56
  176.0 175.1 %all-gather.3.cloned.1.call-start = ((), (), s32[]{:S(2)}) async-start(), calls=%async_computation.6 | async-start | bytes 1671168 | tf_op jit(solution)/shard_map/all_gather | solution.py:61
  251.7 120.3 %reduce-scatter.14.cloned.1.call-start = ((), (), s32[]{:S(2)}) async-start(), calls=%async_computation.10 | async-start | bytes 245760 | tf_op jit(solution)/shard_map/reduce_scatter | solution.py:91
  309.2 82.9 %reduce-scatter.10.cloned.1.call-start = ((), (), s32[]{:S(2)}) async-start(), calls=%async_computation.7 | async-start | bytes 7077888 | tf_op jit(solution)/shard_map/reduce_scatter | solution.py:68
  356.0 1.9 copy-start.1
  356.1 55.2 %reduce-scatter.12.cloned.1.call-start = ((), (), s32[]{:S(2)}) async-start(), calls=%async_computation.9 | async-start | bytes 7077888 | tf_op jit(solution)/shard_map/reduce_scatter | solution.py:71
  365.2 6.9 %copy-start.3 = (f32[384]{0:T(512)S(1)}, f32[384]{0:T(512)}, u32[]{:S(2)}) copy-start(f32[384]{0:T(512)} %param.18) | copy-start | bytes 4612
  367.9 43.3 %copy-start = (bf16[6144,192]{0,1:T(8,128)(2,1)S(1)}, bf16[6144,192]{0,1:T(8,128)(2,1)}, u32[]{:S(2)}) copy-start(bf16[6144,192]{0,1:T(8,128)(2,1)} %copy.18) | copy-start | bytes 7077892
Sparse Core Ops, SparseCore 0:
  81.5 92.6 reduce-scatter.7
  177.4 72.4 reduce-scatter.15
  252.0 52.6 all-gather.4
  306.7 44.3 all-gather.2
  353.3 18.6 reduce-scatter.13
  374.4 17.6 reduce-scatter.9
  394.6 16.6 reduce-scatter.11
where the time goes:
time: 551 us; the launch traced here: 550 us
  waiting for transfers between devices  292 us (53%)
  blocking collectives  193 us (35%)
  matrix products  23.8 us (4%)
  between operations  14.2 us (3%)
  other arithmetic  14 us (3%)
  local copies, waits for them, and re-layouts  12.4 us (2%)
    psum x1, blocking collectives, local(): saliency = lax.psum(terms, ('dp', 'col')) / D  129 us
    reduce_scatter x1, waiting for transfers between devices, local(): lax.psum_scatter(partial_pre, 'col', scatter_dimension=1, tiled=True)  85.5 us
    unnamed x8, waiting for transfers between devices  74 us
    all_gather x1, waiting for transfers between devices, local(): act_all = lax.all_gather(act_share, 'col', axis=1, tiled=True)  52.4 us
    all_gather x1, waiting for transfers between devices, local(): grad_pre = lax.all_gather(grad_pre_share, 'col', axis=1, tiled=True)  41.8 us
    psum x1, blocking collectives, local(): mean_val = lax.psum(jnp.sum(joined, axis=1, keepdims=True), 'col') / D  35.5 us
    psum x1, blocking collectives, local(): lax.psum(jnp.sum(centred * centred, axis=1, keepdims=True), 'col') / D  28.5 us
    reduce_scatter x1, waiting for transfers between devices, local(): lax.psum_scatter(local_in.astype(jnp.bfloat16), 'dp', scatter_dimension=0...  18.7 us
  transfers between devices with their start and end apart: 7, of which 7 were waited for; matrix products, arithmetic and copies ran while one was open for 6% of the time, Pallas kernels for 0%

commit v1 on v0

--- a/solution.py
+++ b/solution.py
@@ -81,7 +81,7 @@
     terms = jnp.sum(jnp.abs(weight_in_rows * summed_in), axis=0) + jnp.sum(
         jnp.abs(weight_out_cols * summed_out), axis=1
     )
-    saliency = lax.psum(terms, ("dp", "col")) / D
+    saliency = lax.psum(lax.psum(terms, "col"), "dp") / D
     neuron_ids = lax.axis_index("row") * neurons_local + jnp.arange(neurons_local, dtype=jnp.int32)
     is_pruned = jnp.any(pruned[:, None] == neuron_ids[None, :], axis=0)
     keep = jnp.where(is_pruned, 0.0, 1.0).astype(jnp.bfloat16)

time: 551 us -> 500 us (0.907)
  blocking collectives: 193 us -> 142 us
    psum x1 -> x2, blocking collectives: 129 us -> 78.1 us  [local(): saliency = lax.psum(lax.psum(terms, 'col'), 'dp') / D]
  transfers between devices with their start and end apart: 7 -> 7, of which waited for: 7 -> 7; matrix products, arithmetic and copies ran while one was open for 6% -> 7% of each run, Pallas kernels for 0% -> 0%
where the time goes in v1:
time: 500 us; the launch traced here: 499 us
  waiting for transfers between devices  292 us (58%)
  blocking collectives  142 us (28%)
  matrix products  23.8 us (5%)
  between operations  14.2 us (3%)
  other arithmetic  14 us (3%)
  local copies, waits for them, and re-layouts  12.4 us (2%)
    reduce_scatter x1, waiting for transfers between devices, local(): lax.psum_scatter(partial_pre, 'col', scatter_dimension=1, tiled=True)  85.5 us
    psum x2, blocking collectives, local(): saliency = lax.psum(lax.psum(terms, 'col'), 'dp') / D  78.1 us
    unnamed x8, waiting for transfers between devices  74 us
    all_gather x1, waiting for transfers between devices, local(): act_all = lax.all_gather(act_share, 'col', axis=1, tiled=True)  52.4 us
    all_gather x1, waiting for transfers between devices, local(): grad_pre = lax.all_gather(grad_pre_share, 'col', axis=1, tiled=True)  41.8 us
    psum x1, blocking collectives, local(): mean_val = lax.psum(jnp.sum(joined, axis=1, keepdims=True), 'col') / D  35.5 us
    psum x1, blocking collectives, local(): lax.psum(jnp.sum(centred * centred, axis=1, keepdims=True), 'col') / D  28.5 us
    reduce_scatter x1, waiting for transfers between devices, local(): lax.psum_scatter(local_in.astype(jnp.bfloat16), 'dp', scatter_dimension=0...  18.7 us
  transfers between devices with their start and end apart: 7, of which 7 were waited for; matrix products, arithmetic and copies ran while one was open for 7% of the time, Pallas kernels for 0%

profile of v1, /device:TPU:1, one launch (start us, length us, event | category | flops | bytes accessed | tf_op | source)
XLA Modules:
  0.0 499.3 jit_solution(684820837986323610)
XLA Ops:
  7.2 0.0 reduce-scatter.8.cloned.1.call-start
  7.2 1.1 convert_reduce_fusion
  8.3 35.5 %psum.28 = f32[256,1]{0,1:T(1,128)S(1)} all-reduce(f32[256,1]{0,1:T(1,128)S(1)} %bitcast.16), channel_id=1, replica_groups=mesh['dp'=2,'row'=4,'col'=16] {'col'}, use_global_device_ids=true, to_apply=%region_1.0 | all-reduce | flops 256 | bytes 2048 | tf_op jit(solution)/shard_map/psum | solution.py:42
  43.8 1.1 fusion.5
  44.9 28.5 %psum.29 = f32[256,1]{0,1:T(1,128)S(1)} all-reduce(f32[256,1]{0,1:T(1,128)S(1)} %bitcast.17), channel_id=1, replica_groups=mesh['dp'=2,'row'=4,'col'=16] {'col'}, use_global_device_ids=true, to_apply=%region_3.0 | all-reduce | flops 256 | bytes 2048 | tf_op jit(solution)/shard_map/psum | solution.py:44
  73.5 1.1 fusion.7
  74.6 6.8 %fusion.19 = f32[256,6144]{1,0:T(8,128)} fusion(bf16[256,384]{1,0:T(8,128)(2,1)S(1)} %fusion.7, bf16[384,6144]{1,0:T(8,128)(2,1)} %param.15), kind=kOutput, calls=%fused_computation.39 | convolution fusion | flops 1207959552 | bytes 11206656 | tf_op jit(solution)/shard_map/dot_general | solution.py:46
  81.4 0.0 reduce-scatter.8.cloned.1.call-update
  81.4 0.0 reduce-scatter.16.cloned.1.call-start
  81.4 0.6 copy-done.5
  82.0 0.2 copy-done.2
  82.3 3.9 convolution_convert_fusion.2
  86.2 1.7 copy.16
  87.9 0.0 reduce-scatter.16.cloned.1.call-update
  87.9 0.0 all-gather.5.cloned.1.call-start
  88.0 0.8 dynamic_slice.10
  88.8 85.5 %reduce-scatter.8.cloned.1.call-done = f32[256,384]{1,0:T(8,128)} async-done(((f32[256,6144]{1,0:T(8,128)}), f32[256,384]{1,0:T(8,128)}) %reduce-scatter.8.cloned.1.call-update) | async-done | bytes 393232 | tf_op jit(solution)/shard_map/reduce_scatter | solution.py:54
  174.2 1.8 multiply_convert_fusion
  176.0 0.0 all-gather.5.cloned.1.call-update
  176.0 0.0 all-gather.3.cloned.1.call-start
  176.1 73.9 %reduce-scatter.16.cloned.1.call-done = bf16[384,128]{1,0:T(8,128)(2,1)} async-done(((bf16[6144,128]{1,0:T(8,128)(2,1)}), bf16[384,128]{1,0:T(8,128)(2,1)}) %reduce-scatter.16.cloned.1.call-update) | async-done | bytes 98320
  249.9 1.0 copy.17
  250.9 0.7 fusion.13
  251.7 0.0 all-gather.3.cloned.1.call-update
  251.7 0.0 reduce-scatter.14.cloned.1.call-start
  251.8 0.5 compare_reduce_fusion
  252.3 52.4 %all-gather.5.cloned.1.call-done = bf16[256,6144]{1,0:T(8,128)(2,1)} async-done(((bf16[256,384]{1,0:T(8,128)(2,1)}), bf16[256,6144]{1,0:T(8,128)(2,1)}) %all-gather.5.cloned.1.call-update) | async-done | bytes 3145744 | tf_op jit(solution)/shard_map/all_gather | solution.py:56
  304.7 4.5 fusion
  309.2 0.0 reduce-scatter.14.cloned.1.call-update
  309.2 0.0 reduce-scatter.10.cloned.1.call-start
  309.3 41.8 %all-gather.3.cloned.1.call-done = bf16[128,6144]{1,0:T(8,128)(2,1)} async-done(((bf16[128,384]{1,0:T(8,128)(2,1)}), bf16[128,6144]{1,0:T(8,128)(2,1)}) %all-gather.3.cloned.1.call-update) | async-done | bytes 1572880 | tf_op jit(solution)/shard_map/all_gather | solution.py:61
  351.1 4.9 convolution_convert_fusion.1
  356.0 0.0 reduce-scatter.10.cloned.1.call-update
  356.1 0.0 reduce-scatter.12.cloned.1.call-start
  356.1 1.8 copy-done.1
  357.9 3.7 convolution_convert_fusion
  361.6 0.0 reduce-scatter.12.cloned.1.call-update
  361.6 3.6 constant_dynamic-slice_fusion
  365.2 2.7 copy.18
  367.9 4.1 reduce-scatter.14.cloned.1.call-done
  372.0 1.4 add_convert_fusion
  373.4 18.7 %reduce-scatter.10.cloned.1.call-done = bf16[192,6144]{1,0:T(8,128)(2,1)} async-done(((bf16[384,6144]{1,0:T(8,128)(2,1)}), bf16[192,6144]{1,0:T(8,128)(2,1)}) %reduce-scatter.10.cloned.1.call-update) | async-done | bytes 2359312 | tf_op jit(solution)/shard_map/reduce_scatter | solution.py:68
  392.2 3.2 abs_reduce_fusion.1
  395.3 15.9 %reduce-scatter.12.cloned.1.call-done = bf16[6144,192]{0,1:T(8,128)(2,1)} async-done(((bf16[6144,384]{0,1:T(8,128)(2,1)}), bf16[6144,192]{0,1:T(8,128)(2,1)}) %reduce-scatter.12.cloned.1.call-update) | async-done | bytes 2359312 | tf_op jit(solution)/shard_map/reduce_scatter | solution.py:71
  411.2 2.5 abs_reduce_fusion
  413.7 60.8 %psum.30 = f32[6144]{0:T(1024)S(1)} all-reduce(f32[6144]{0:T(1024)S(1)} %add.86), channel_id=1, replica_groups=mesh['dp'=2,'row'=4,'col'=16] {'col'}, use_global_device_ids=true, to_apply=%region_10.0 | all-reduce | flops 6144 | bytes 49152 | tf_op jit(solution)/shard_map/psum | solution.py:84
  474.5 17.4 %psum.31 = f32[6144]{0:T(1024)S(1)} all-reduce(f32[6144]{0:T(1024)S(1)} %psum.30), channel_id=1, replica_groups=mesh['dp'=2,'row'=4,'col'=16] {'dp'}, use_global_device_ids=true, to_apply=%region_11.0 | all-reduce | flops 6144 | bytes 49152 | tf_op jit(solution)/shard_map/psum | solution.py:84
  491.8 0.6 broadcast_multiply_fusion
  (15 shorter events, 0.1 us)
Async XLA Ops:
  7.2 167.1 %reduce-scatter.8.cloned.1.call-start = ((), (), s32[]{:S(2)}) async-start(), calls=%async_computation.5 | async-start | bytes 6684672 | tf_op jit(solution)/shard_map/reduce_scatter | solution.py:54
  81.4 0.7 copy-start.5
  81.4 0.9 copy-start.2
  81.4 168.5 %reduce-scatter.16.cloned.1.call-start = ((), (), s32[]{:S(2)}) async-start(), calls=%async_computation.11 | async-start | bytes 1671168
  86.2 165.5 %copy-start.4 = (s32[128]{0:T(128)S(1)}, s32[128]{0:T(128)}, u32[]{:S(2)}) copy-start(s32[128]{0:T(128)} %param.19) | copy-start | bytes 1540
  87.9 216.8 %all-gather.5.cloned.1.call-start = ((), (), s32[]{:S(2)}) async-start(), calls=%async_computation.8 | async-start | bytes 3342336 | tf_op jit(solution)/shard_map/all_gather | solution.py:56
  176.0 175.1 %all-gather.3.cloned.1.call-start = ((), (), s32[]{:S(2)}) async-start(), calls=%async_computation.6 | async-start | bytes 1671168 | tf_op jit(solution)/shard_map/all_gather | solution.py:61
  251.7 120.3 %reduce-scatter.14.cloned.1.call-start = ((), (), s32[]{:S(2)}) async-start(), calls=%async_computation.10 | async-start | bytes 245760 | tf_op jit(solution)/shard_map/reduce_scatter | solution.py:91
  309.2 82.9 %reduce-scatter.10.cloned.1.call-start = ((), (), s32[]{:S(2)}) async-start(), calls=%async_computation.7 | async-start | bytes 7077888 | tf_op jit(solution)/shard_map/reduce_scatter | solution.py:68
  356.0 1.9 copy-start.1
  356.1 55.2 %reduce-scatter.12.cloned.1.call-start = ((), (), s32[]{:S(2)}) async-start(), calls=%async_computation.9 | async-start | bytes 7077888 | tf_op jit(solution)/shard_map/reduce_scatter | solution.py:71
  365.2 6.9 %copy-start.3 = (f32[384]{0:T(512)S(1)}, f32[384]{0:T(512)}, u32[]{:S(2)}) copy-start(f32[384]{0:T(512)} %param.18) | copy-start | bytes 4612
  367.9 43.3 %copy-start = (bf16[6144,192]{0,1:T(8,128)(2,1)S(1)}, bf16[6144,192]{0,1:T(8,128)(2,1)}, u32[]{:S(2)}) copy-start(bf16[6144,192]{0,1:T(8,128)(2,1)} %copy.18) | copy-start | bytes 7077892
Sparse Core Ops, SparseCore 0:
  81.5 92.6 reduce-scatter.7
  177.4 72.4 reduce-scatter.15
  252.0 52.6 all-gather.4
  306.7 44.3 all-gather.2
  353.3 18.6 reduce-scatter.13
  374.4 17.6 reduce-scatter.9
  394.6 16.6 reduce-scatter.11
